TPU v7x, 32 devices: a whole 2x2x4 slice. The times are simulated.
32 devices in a mesh: row: 16 (over z, y, x), col: 2 (over core).
Axes of the slice: x: 2, y: 2, z: 4, core: 2. Of those that a mesh axis runs over, the one named last changes fastest.
Arguments:
- blocks: float32 [16, 2, 40, 128, 128], P('row', 'col'), may hold values from -0.078125 to 0.078125
- block_rows: int32 [16, 2, 40], P('row', 'col'), may hold values from 0 to 15
- block_cols: int32 [16, 2, 40], P(None, 'col'), may hold values from 0 to 127, as said below
- start_basis: float32 [32, 32768], P(None, ('row', 'col')), may hold values from -6 to 6
- targets: int32 [16], replicated, may hold values from 0 to 31, as said below
Outputs:
- right_basis: float32 [32, 32768], P(None, ('row', 'col'))
- left_basis: float32 [32, 32768], P(None, ('row', 'col'))
- triangle: float32 [32, 32], replicated
Inputs may be any that keep to these rules, and one draw needn't show every extreme that they name: For every r, c and o < 16, all entries block_cols[r, c, n] with block_cols[r, c, n] // 8 = o are equal. `targets`: 16 distinct indices.
All inputs are finite; a program needn't handle non-finite values.
Results may differ from a plain program's by a relative error of at most 0.0001.
Values sent between devices are 32-bit elements; how exact they have to be, the bound alone decides.
No kernel may reach another device: no remote copies, remote signals or barrier semaphores. Data moves between devices by JAX's collectives and lax.ppermute only.
A program may use at most 64 MiB of HBM per device.

v0:
```python
import jax
import jax.numpy as jnp
from jax import lax
from jax.sharding import PartitionSpec as P

OUTER = 2
INNER = 4
highest = lax.Precision.HIGHEST


def lower_solve(lower, vectors):
    return lax.linalg.triangular_solve(lower, vectors, left_side=True, lower=True)


def gram_local(vectors):
    return jnp.dot(vectors, vectors.T, precision=highest)


def basis_factor(trial_basis, total_rows):
    gram_sum = lax.psum(gram_local(trial_basis), ("row", "col"))
    return jnp.linalg.cholesky(gram_sum / total_rows)


def multiply(vectors, block_tiles, tables):
    pick_hot, owners_mine, owner_hot, row_hot, rows_local = tables
    count_vectors = vectors.shape[0]
    block_size = block_tiles.shape[-1]
    segments = vectors.reshape(count_vectors, -1, block_size)
    outgoing = jnp.einsum("rt,ktb->rkb", pick_hot, segments, precision=highest)
    incoming = lax.all_to_all(outgoing, "row", split_axis=0, concat_axis=0, tiled=True)
    picked = incoming[owners_mine]
    products = jnp.einsum("nij,nkj->kni", block_tiles, picked, precision=highest)
    partial_value = jnp.einsum("nr,kni->kri", row_hot, products, precision=highest).reshape(
        count_vectors, -1
    )
    own_rows = lax.psum_scatter(partial_value, "col", scatter_dimension=1, tiled=True)
    result = (own_rows, own_rows)
    return result


def multiply_back(left_rows, block_tiles, tables):
    pick_hot, owners_mine, owner_hot, row_hot, rows_local = tables
    count_vectors = left_rows.shape[0]
    block_size = block_tiles.shape[-1]
    segments = left_rows.reshape(count_vectors, -1, block_size)
    picked = segments[:, rows_local]
    products = jnp.einsum("nij,kni->knj", block_tiles, picked, precision=highest)
    outgoing = jnp.einsum("no,knj->okj", owner_hot, products, precision=highest)
    incoming = lax.all_to_all(outgoing, "row", split_axis=0, concat_axis=0, tiled=True)
    returned = jnp.einsum("rt,rkb->ktb", pick_hot, incoming, precision=highest)
    return returned.reshape(count_vectors, -1)


def shards(blocks, block_rows, block_cols, start_basis, targets):
    block_size = blocks.shape[-1]
    block_tiles = blocks.reshape(-1, block_size, block_size)
    rows_local = block_rows.reshape(-1)
    row_count = lax.axis_size("row")
    col_count = lax.axis_size("col")
    own_width = start_basis.shape[1]
    seg_count = own_width // block_size
    total_rows = float(own_width * row_count * col_count)
    count_vectors = start_basis.shape[0]
    pattern = block_cols[:, 0, :]
    me_row = lax.axis_index("row")
    cols_local = lax.dynamic_index_in_dim(pattern, me_row, 0, keepdims=False)
    owners_mine = cols_local // seg_count
    seg_ids = jnp.arange(seg_count, dtype=jnp.int32)
    matched = pattern // seg_count == me_row
    within = pattern % seg_count
    pick_hot = jnp.any(
        matched[:, :, None] & (within[:, :, None] == seg_ids[None, None, :]), axis=1
    ).astype(jnp.float32)
    owner_hot = (owners_mine[:, None] == jnp.arange(row_count, dtype=jnp.int32)[None, :]).astype(
        jnp.float32
    )
    row_hot = (
        rows_local[:, None] == jnp.arange(col_count * seg_count, dtype=jnp.int32)[None, :]
    ).astype(jnp.float32)
    col_hot = (
        cols_local[:, None] == jnp.arange(row_count * seg_count, dtype=jnp.int32)[None, :]
    ).astype(jnp.float32)
    tables = (pick_hot, owners_mine, owner_hot, row_hot, rows_local)
    squared = jnp.sum(block_tiles * block_tiles, axis=1)
    column_terms = jnp.dot(col_hot.T, squared, precision=highest).reshape(-1)
    squares = lax.psum_scatter(column_terms, "row", scatter_dimension=0, tiled=True)
    largest = lax.pmax(jnp.max(squares), ("row", "col"))
    chosen = jnp.sum(
        (targets[None, :] == jnp.arange(count_vectors, dtype=jnp.int32)[:, None]).astype(
            jnp.float32
        ),
        axis=1,
    )
    trial_basis = start_basis
    left_own = start_basis
    lower_image = jnp.zeros((count_vectors, count_vectors), jnp.float32)
    for outer_step in range(OUTER):
        lower_basis = basis_factor(trial_basis, total_rows)
        right_now = lower_solve(lower_basis, trial_basis)
        image_own, image_rows = multiply(right_now, block_tiles, tables)
        gram_image = lax.psum(gram_local(image_own), ("row", "col"))
        lower_image = jnp.linalg.cholesky(gram_image / total_rows)
        left_own = lower_solve(lower_image, image_own)
        left_rows = lax.all_gather(left_own, "col", axis=1, tiled=True)
        back_own = multiply_back(left_rows, block_tiles, tables)
        residual = back_own - jnp.dot(lower_image.T, right_now, precision=highest)
        shifts = jnp.sum(lower_image * lower_image, axis=1) + largest
        correction = residual / shifts[:, None]
        for inner_step in range(1, INNER):
            coupling = (
                lax.psum(
                    jnp.dot(right_now, (squares[None, :] * correction).T, precision=highest),
                    ("row", "col"),
                )
                / total_rows
            )
            correction = (
                residual
                + squares[None, :] * correction
                - jnp.dot(coupling.T, right_now, precision=highest)
            ) / shifts[:, None]
        trial_basis = right_now + chosen[:, None] * correction
    lower_basis = basis_factor(trial_basis, total_rows)
    return (lower_solve(lower_basis, trial_basis), left_own, lower_image.T)


def solution(mesh):
    in_specs = (
        P("row", "col", None, None, None),
        P("row", "col", None),
        P(None, "col", None),
        P(None, ("row", "col")),
        P(),
    )
    out_specs = (P(None, ("row", "col")), P(None, ("row", "col")), P())
    return jax.shard_map(shards, mesh=mesh, in_specs=in_specs, out_specs=out_specs, check_vma=False)
```

profile of v0, /device:TPU:0, one launch (start us, length us, event | category | flops | bytes accessed | tf_op | source)
XLA Modules:
  0.0 756.0 jit_solution(7076702651899851333)
XLA Ops:
  9.9 42.1 %psum.77 = f32[32,32]{0,1:T(8,128)S(1)} all-reduce(f32[32,32]{0,1:T(8,128)S(1)} %fusion.142), channel_id=1, replica_groups=mesh['row'=16,'col'=2] {'row','col'}, use_global_device_ids=true, to_apply=%region_0.1 | all-reduce | flops 1024 | bytes 8192 | tf_op jit(solution)/shard_map/psum | solution.py:20
  60.5 5.4 all-to-all-start
  67.3 7.6 %all-to-all-done = f32[16,32,128]{2,1,0:T(8,128)S(1)} async-done(((f32[16,32,128]{2,1,0:T(8,128)}), f32[16,32,128]{2,1,0:T(8,128)S(1)}, u32[]{:S(2)}, u32[]{:S(2)}) %all-to-all-start) | async-done | bytes 262176 | tf_op jit(solution)/shard_map/all_to_all | solution.py:30
  76.4 5.2 fusion.9
  83.5 5.5 reduce-scatter.3.cloned.1.call-done
  90.2 40.5 %psum.78 = f32[32,32]{0,1:T(8,128)S(1)} all-reduce(f32[32,32]{0,1:T(8,128)S(1)} %fusion.143), channel_id=1, replica_groups=mesh['row'=16,'col'=2] {'row','col'}, use_global_device_ids=true, to_apply=%region_6.9 | all-reduce | flops 1024 | bytes 8192 | tf_op jit(solution)/shard_map/psum | solution.py:101
  142.5 3.5 fusion.12
  147.5 5.4 all-to-all-start.1
  155.4 108.3 %all-reduce.3.cloned.1.call-done = f32[16384]{0:T(1024)} async-done(((f32[16384]{0:T(1024)}), f32[16384]{0:T(1024)}) %all-reduce.3.cloned.1.call-update) | async-done | bytes 65552
  265.0 39.7 %pmax.7 = f32[]{:T(128)} all-reduce(f32[]{:T(128)} %get-tuple-element.23), channel_id=1, replica_groups=mesh['row'=16,'col'=2] {'row','col'}, use_global_device_ids=true, to_apply=%region_11.14 | all-reduce | flops 1 | bytes 8 | tf_op jit(solution)/shard_map/pmax | solution.py:87
  307.0 39.9 %psum.79 = f32[32,32]{0,1:T(8,128)S(1)} all-reduce(f32[32,32]{0,1:T(8,128)S(1)} %fusion.49), channel_id=1, replica_groups=mesh['row'=16,'col'=2] {'row','col'}, use_global_device_ids=true, to_apply=%region_12.15 | all-reduce | flops 1024 | bytes 8192 | tf_op jit(solution)/shard_map/psum | solution.py:111
  347.5 40.4 %psum.80 = f32[32,32]{0,1:T(8,128)S(1)} all-reduce(f32[32,32]{0,1:T(8,128)S(1)} %fusion.144), channel_id=1, replica_groups=mesh['row'=16,'col'=2] {'row','col'}, use_global_device_ids=true, to_apply=%region_13.16 | all-reduce | flops 1024 | bytes 8192 | tf_op jit(solution)/shard_map/psum | solution.py:111
  388.4 39.8 %psum.81 = f32[32,32]{0,1:T(8,128)S(1)} all-reduce(f32[32,32]{0,1:T(8,128)S(1)} %fusion.145), channel_id=1, replica_groups=mesh['row'=16,'col'=2] {'row','col'}, use_global_device_ids=true, to_apply=%region_14.17 | all-reduce | flops 1024 | bytes 8192 | tf_op jit(solution)/shard_map/psum | solution.py:111
  428.8 40.3 %psum.82 = f32[32,32]{0,1:T(8,128)S(1)} all-reduce(f32[32,32]{0,1:T(8,128)S(1)} %fusion.146), channel_id=1, replica_groups=mesh['row'=16,'col'=2] {'row','col'}, use_global_device_ids=true, to_apply=%region_15.18 | all-reduce | flops 1024 | bytes 8192 | tf_op jit(solution)/shard_map/psum | solution.py:20
  476.6 13.9 %all_to_all.20 = f32[16,32,128]{2,1,0:T(8,128)S(1)} all-to-all(f32[16,32,128]{2,1,0:T(8,128)S(1)} %copy.137), channel_id=1, replica_groups=mesh['row'=16,'col'=2] {'row'}, dimensions={0} | all-to-all | bytes 524288 | tf_op jit(solution)/shard_map/all_to_all | solution.py:30
  491.9 5.2 fusion.15
  498.7 5.8 reduce-scatter.5.cloned.1.call-done
  505.8 40.5 %psum.83 = f32[32,32]{0,1:T(8,128)S(1)} all-reduce(f32[32,32]{0,1:T(8,128)S(1)} %fusion.147), channel_id=1, replica_groups=mesh['row'=16,'col'=2] {'row','col'}, use_global_device_ids=true, to_apply=%region_17.20 | all-reduce | flops 1024 | bytes 8192 | tf_op jit(solution)/shard_map/psum | solution.py:101
  562.8 5.4 all-to-all-start.3
  569.6 8.8 %all-to-all-done.3 = f32[16,32,128]{2,1,0:T(8,128)S(1)} async-done(((f32[16,32,128]{2,1,0:T(8,128)}), f32[16,32,128]{2,1,0:T(8,128)S(1)}, u32[]{:S(2)}, u32[]{:S(2)}) %all-to-all-start.3) | async-done | bytes 262176 | tf_op jit(solution)/shard_map/all_to_all | solution.py:49
  580.1 38.9 %psum.84 = f32[32,32]{0,1:T(8,128)S(1)} all-reduce(f32[32,32]{0,1:T(8,128)S(1)} %fusion.50), channel_id=1, replica_groups=mesh['row'=16,'col'=2] {'row','col'}, use_global_device_ids=true, to_apply=%region_19.22 | all-reduce | flops 1024 | bytes 8192 | tf_op jit(solution)/shard_map/psum | solution.py:111
  619.5 39.9 %psum.85 = f32[32,32]{0,1:T(8,128)S(1)} all-reduce(f32[32,32]{0,1:T(8,128)S(1)} %fusion.148), channel_id=1, replica_groups=mesh['row'=16,'col'=2] {'row','col'}, use_global_device_ids=true, to_apply=%region_20.23 | all-reduce | flops 1024 | bytes 8192 | tf_op jit(solution)/shard_map/psum | solution.py:111
  659.9 40.5 %psum.86 = f32[32,32]{0,1:T(8,128)S(1)} all-reduce(f32[32,32]{0,1:T(8,128)S(1)} %fusion.149), channel_id=1, replica_groups=mesh['row'=16,'col'=2] {'row','col'}, use_global_device_ids=true, to_apply=%region_21.24 | all-reduce | flops 1024 | bytes 8192 | tf_op jit(solution)/shard_map/psum | solution.py:111
  700.9 39.9 %psum.87 = f32[32,32]{0,1:T(8,128)S(1)} all-reduce(f32[32,32]{0,1:T(8,128)S(1)} %fusion.150), channel_id=1, replica_groups=mesh['row'=16,'col'=2] {'row','col'}, use_global_device_ids=true, to_apply=%region_22.25 | all-reduce | flops 1024 | bytes 8192 | tf_op jit(solution)/shard_map/psum | solution.py:20
  (124 shorter events, 76.6 us)
Async XLA Ops:
  8.0 1.6 copy-start
  8.0 68.4 %copy-start.1 = (f32[1,1,40,128,128]{4,3,2,1,0:T(8,128)S(1)}, f32[1,1,40,128,128]{4,3,2,1,0:T(8,128)}, u32[]{:S(2)}) copy-start(f32[1,1,40,128,128]{4,3,2,1,0:T(8,128)} %param.8) | copy-start | bytes 7864324
  60.5 14.5 %all-to-all-start = ((f32[16,32,128]{2,1,0:T(8,128)}), f32[16,32,128]{2,1,0:T(8,128)S(1)}, u32[]{:S(2)}, u32[]{:S(2)}) async-start(f32[16,32,128]{2,1,0:T(8,128)} %copy.122), calls=%async_computation | async-start | bytes 524288 | tf_op jit(solution)/shard_map/all_to_all | solution.py:30
  65.9 23.1 %reduce-scatter.3.cloned.1.call-start = ((), (), s32[]{:S(2)}) async-start(), calls=%async_computation.6 | async-start | bytes 393216 | tf_op jit(solution)/shard_map/reduce_scatter | solution.py:36
  67.3 14.3 %copy-start.3 = (s32[1,1,40]{2,1,0:T(1,128)S(1)}, s32[1,1,40]{2,1,0:T(1,128)}, u32[]{:S(2)}) copy-start(s32[1,1,40]{2,1,0:T(1,128)} %param.9) | copy-start | bytes 484
  142.5 11.5 %copy-start.5 = (u32[32]{0:T(128)S(1)}, u32[32]{0:T(128)}, u32[]{:S(2)}) copy-start(u32[32]{0:T(128)} %constant.104) | copy-start | bytes 388
  142.5 12.7 %copy-start.4 = (s32[16]{0:T(128)S(1)}, s32[16]{0:T(128)}, u32[]{:S(2)}) copy-start(s32[16]{0:T(128)} %param.12) | copy-start | bytes 196
  147.5 157.9 %all-to-all-start.1 = ((f32[16,32,128]{2,1,0:T(8,128)}), f32[16,32,128]{2,1,0:T(8,128)S(1)}, u32[]{:S(2)}, u32[]{:S(2)}) async-start(f32[16,32,128]{2,1,0:T(8,128)} %copy.128), calls=%async_computation.2 | async-start | bytes 524288 | tf_op jit(solution)/shard_map/all_to_all | solution.py:49
  152.9 110.8 %all-reduce.3.cloned.1.call-start = ((), (), s32[]{:S(2)}) async-start(), calls=%async_computation.8 | async-start | bytes 131072
  154.0 350.6 %reduce-scatter.5.cloned.1.call-start = ((), (), s32[]{:S(2)}) async-start(), calls=%async_computation.7 | async-start | bytes 393216 | tf_op jit(solution)/shard_map/reduce_scatter | solution.py:36
  554.4 6.9 copy-start.2
  562.8 15.6 %all-to-all-start.3 = ((f32[16,32,128]{2,1,0:T(8,128)}), f32[16,32,128]{2,1,0:T(8,128)S(1)}, u32[]{:S(2)}, u32[]{:S(2)}) async-start(f32[16,32,128]{2,1,0:T(8,128)} %copy.143), calls=%async_computation.5 | async-start | bytes 524288 | tf_op jit(solution)/shard_map/all_to_all | solution.py:49
Sparse Core Ops, SparseCore 0:
  83.3 5.6 reduce-scatter.2
  498.8 5.6 reduce-scatter.4
Sparse Core Ops, SparseCore 1:
  159.5 104.2 all-reduce.2
where the time goes:
time: 759 us; the launch traced here: 756 us
  blocking collectives  501 us (66%)
  waiting for transfers between devices  136 us (18%)
  other arithmetic  39.9 us (5%)
  matrix products  34.9 us (5%)
  between operations  16.6 us (2%)
  starting transfers between devices  16.5 us (2%)
  local copies, waits for them, and re-layouts  11.4 us (2%)
    psum x6, blocking collectives, shards(): lax.psum(jnp.dot(right_now, (squares[None, :] * correction).T, precision=...  239 us
    psum x3, blocking collectives, basis_factor(): gram_sum = lax.psum(gram_local(trial_basis), ('row', 'col'))  122 us
    unnamed x4, waiting for transfers between devices  108 us
    psum x2, blocking collectives, shards(): gram_image = lax.psum(gram_local(image_own), ('row', 'col'))  81 us
    pmax x1, blocking collectives, shards(): largest = lax.pmax(jnp.max(squares), ('row', 'col'))  39.7 us
  transfers between devices with their start and end apart: 6, of which 5 were waited for; matrix products, arithmetic and copies ran while one was open for 1% of the time, Pallas kernels for 0%

commit v1 on v0

--- a/solution.py
+++ b/solution.py
@@ -98,7 +98,8 @@
         lower_basis = basis_factor(trial_basis, total_rows)
         right_now = lower_solve(lower_basis, trial_basis)
         image_own, image_rows = multiply(right_now, block_tiles, tables)
-        gram_image = lax.psum(gram_local(image_own), ("row", "col"))
+        inner = lax.psum(gram_local(image_own), "col")
+        gram_image = lax.psum(inner, "row")
         lower_image = jnp.linalg.cholesky(gram_image / total_rows)
         left_own = lower_solve(lower_image, image_own)
         left_rows = lax.all_gather(left_own, "col", axis=1, tiled=True)

time: 759 us -> 834 us (1.099)
  blocking collectives: 501 us -> 580 us
    psum x2 -> x4, blocking collectives: 81 us -> 161 us  [the longest x2 154 us: shards(): gram_image = lax.psum(inner, 'row')]
where the time goes in v1:
time: 834 us; the launch traced here: 832 us
  blocking collectives  580 us (70%)
  waiting for transfers between devices  136 us (16%)
  other arithmetic  39.9 us (5%)
  matrix products  34.9 us (4%)
  between operations  16.6 us (2%)
  starting transfers between devices  12.8 us (2%)
  local copies, waits for them, and re-layouts  11.4 us (1%)
    psum x6, blocking collectives, shards(): lax.psum(jnp.dot(right_now, (squares[None, :] * correction).T, precision=...  239 us
    psum x2, blocking collectives, shards(): gram_image = lax.psum(inner, 'row')  154 us
    psum x3, blocking collectives, basis_factor(): gram_sum = lax.psum(gram_local(trial_basis), ('row', 'col'))  122 us
    unnamed x4, waiting for transfers between devices  108 us
    pmax x1, blocking collectives, shards(): largest = lax.pmax(jnp.max(squares), ('row', 'col'))  39.7 us
  transfers between devices with their start and end apart: 6, of which 5 were waited for; matrix products, arithmetic and copies ran while one was open for 1% of the time, Pallas kernels for 0%

profile of v1, /device:TPU:0, one launch (start us, length us, event | category | flops | bytes accessed | tf_op | source)
XLA Modules:
  0.0 831.9 jit_solution(4133370503937087205)
XLA Ops:
  9.9 42.1 %psum.91 = f32[32,32]{0,1:T(8,128)S(1)} all-reduce(f32[32,32]{0,1:T(8,128)S(1)} %fusion.142), channel_id=1, replica_groups=mesh['row'=16,'col'=2] {'row','col'}, use_global_device_ids=true, to_apply=%region_0.1 | all-reduce | flops 1024 | bytes 8192 | tf_op jit(solution)/shard_map/psum | solution.py:20
  60.5 5.4 all-to-all-start
  67.3 7.6 all-to-all-done
  76.4 5.2 fusion.9
  83.5 5.5 reduce-scatter.3.cloned.1.call-done
  93.6 77.1 %psum.93 = f32[32,32]{0,1:T(8,128)S(1)} all-reduce(f32[32,32]{0,1:T(8,128)S(1)} %psum.92), channel_id=1, replica_groups=mesh['row'=16,'col'=2] {'row'}, use_global_device_ids=true, to_apply=%region_7.10 | all-reduce | flops 1024 | bytes 8192 | tf_op jit(solution)/shard_map/psum | solution.py:102
  182.3 3.5 fusion.12
  187.2 3.5 all-to-all-start.1
  193.4 108.1 %all-reduce.3.cloned.1.call-done = f32[16384]{0:T(1024)} async-done(((f32[16384]{0:T(1024)}), f32[16384]{0:T(1024)}) %all-reduce.3.cloned.1.call-update) | async-done | bytes 65552
  302.8 39.7 %pmax.7 = f32[]{:T(128)} all-reduce(f32[]{:T(128)} %get-tuple-element.23), channel_id=1, replica_groups=mesh['row'=16,'col'=2] {'row','col'}, use_global_device_ids=true, to_apply=%region_12.15 | all-reduce | flops 1 | bytes 8 | tf_op jit(solution)/shard_map/pmax | solution.py:87
  344.9 39.9 %psum.94 = f32[32,32]{0,1:T(8,128)S(1)} all-reduce(f32[32,32]{0,1:T(8,128)S(1)} %fusion.49), channel_id=1, replica_groups=mesh['row'=16,'col'=2] {'row','col'}, use_global_device_ids=true, to_apply=%region_13.16 | all-reduce | flops 1024 | bytes 8192 | tf_op jit(solution)/shard_map/psum | solution.py:112
  385.4 40.4 %psum.95 = f32[32,32]{0,1:T(8,128)S(1)} all-reduce(f32[32,32]{0,1:T(8,128)S(1)} %fusion.144), channel_id=1, replica_groups=mesh['row'=16,'col'=2] {'row','col'}, use_global_device_ids=true, to_apply=%region_14.17 | all-reduce | flops 1024 | bytes 8192 | tf_op jit(solution)/shard_map/psum | solution.py:112
  426.3 39.8 %psum.96 = f32[32,32]{0,1:T(8,128)S(1)} all-reduce(f32[32,32]{0,1:T(8,128)S(1)} %fusion.145), channel_id=1, replica_groups=mesh['row'=16,'col'=2] {'row','col'}, use_global_device_ids=true, to_apply=%region_15.18 | all-reduce | flops 1024 | bytes 8192 | tf_op jit(solution)/shard_map/psum | solution.py:112
  466.6 40.3 %psum.97 = f32[32,32]{0,1:T(8,128)S(1)} all-reduce(f32[32,32]{0,1:T(8,128)S(1)} %fusion.146), channel_id=1, replica_groups=mesh['row'=16,'col'=2] {'row','col'}, use_global_device_ids=true, to_apply=%region_16.19 | all-reduce | flops 1024 | bytes 8192 | tf_op jit(solution)/shard_map/psum | solution.py:20
  514.5 13.9 %all_to_all.20 = f32[16,32,128]{2,1,0:T(8,128)S(1)} all-to-all(f32[16,32,128]{2,1,0:T(8,128)S(1)} %copy.137), channel_id=1, replica_groups=mesh['row'=16,'col'=2] {'row'}, dimensions={0} | all-to-all | bytes 524288 | tf_op jit(solution)/shard_map/all_to_all | solution.py:30
  529.8 5.2 fusion.15
  536.5 5.8 reduce-scatter.5.cloned.1.call-done
  547.0 77.1 %psum.99 = f32[32,32]{0,1:T(8,128)S(1)} all-reduce(f32[32,32]{0,1:T(8,128)S(1)} %psum.98), channel_id=1, replica_groups=mesh['row'=16,'col'=2] {'row'}, use_global_device_ids=true, to_apply=%region_19.22 | all-reduce | flops 1024 | bytes 8192 | tf_op jit(solution)/shard_map/psum | solution.py:102
  640.6 3.5 all-to-all-start.3
  645.5 9.1 %all-to-all-done.3 = f32[16,32,128]{2,1,0:T(8,128)S(1)} async-done(((f32[16,32,128]{2,1,0:T(8,128)}), f32[16,32,128]{2,1,0:T(8,128)S(1)}, u32[]{:S(2)}, u32[]{:S(2)}) %all-to-all-start.3) | async-done | bytes 262176 | tf_op jit(solution)/shard_map/all_to_all | solution.py:49
  656.2 38.9 %psum.100 = f32[32,32]{0,1:T(8,128)S(1)} all-reduce(f32[32,32]{0,1:T(8,128)S(1)} %fusion.50), channel_id=1, replica_groups=mesh['row'=16,'col'=2] {'row','col'}, use_global_device_ids=true, to_apply=%region_21.24 | all-reduce | flops 1024 | bytes 8192 | tf_op jit(solution)/shard_map/psum | solution.py:112
  695.5 39.9 %psum.101 = f32[32,32]{0,1:T(8,128)S(1)} all-reduce(f32[32,32]{0,1:T(8,128)S(1)} %fusion.148), channel_id=1, replica_groups=mesh['row'=16,'col'=2] {'row','col'}, use_global_device_ids=true, to_apply=%region_22.25 | all-reduce | flops 1024 | bytes 8192 | tf_op jit(solution)/shard_map/psum | solution.py:112
  736.0 40.2 %psum.102 = f32[32,32]{0,1:T(8,128)S(1)} all-reduce(f32[32,32]{0,1:T(8,128)S(1)} %fusion.149), channel_id=1, replica_groups=mesh['row'=16,'col'=2] {'row','col'}, use_global_device_ids=true, to_apply=%region_23.26 | all-reduce | flops 1024 | bytes 8192 | tf_op jit(solution)/shard_map/psum | solution.py:112
  776.8 39.9 %psum.103 = f32[32,32]{0,1:T(8,128)S(1)} all-reduce(f32[32,32]{0,1:T(8,128)S(1)} %fusion.150), channel_id=1, replica_groups=mesh['row'=16,'col'=2] {'row','col'}, use_global_device_ids=true, to_apply=%region_24.27 | all-reduce | flops 1024 | bytes 8192 | tf_op jit(solution)/shard_map/psum | solution.py:20
  (126 shorter events, 83.4 us)
Async XLA Ops:
  8.0 1.6 copy-start
  8.0 68.4 %copy-start.1 = (f32[1,1,40,128,128]{4,3,2,1,0:T(8,128)S(1)}, f32[1,1,40,128,128]{4,3,2,1,0:T(8,128)}, u32[]{:S(2)}) copy-start(f32[1,1,40,128,128]{4,3,2,1,0:T(8,128)} %param.8) | copy-start | bytes 7864324
  60.5 14.5 %all-to-all-start = ((f32[16,32,128]{2,1,0:T(8,128)}), f32[16,32,128]{2,1,0:T(8,128)S(1)}, u32[]{:S(2)}, u32[]{:S(2)}) async-start(f32[16,32,128]{2,1,0:T(8,128)} %copy.122), calls=%async_computation | async-start | bytes 524288 | tf_op jit(solution)/shard_map/all_to_all | solution.py:30
  65.9 23.1 %reduce-scatter.3.cloned.1.call-start = ((), (), s32[]{:S(2)}) async-start(), calls=%async_computation.6 | async-start | bytes 393216 | tf_op jit(solution)/shard_map/reduce_scatter | solution.py:36
  67.3 14.3 %copy-start.3 = (s32[1,1,40]{2,1,0:T(1,128)S(1)}, s32[1,1,40]{2,1,0:T(1,128)}, u32[]{:S(2)}) copy-start(s32[1,1,40]{2,1,0:T(1,128)} %param.9) | copy-start | bytes 484
  182.3 9.8 %copy-start.5 = (u32[32]{0:T(128)S(1)}, u32[32]{0:T(128)}, u32[]{:S(2)}) copy-start(u32[32]{0:T(128)} %constant.104) | copy-start | bytes 388
  182.3 11.0 %copy-start.4 = (s32[16]{0:T(128)S(1)}, s32[16]{0:T(128)}, u32[]{:S(2)}) copy-start(s32[16]{0:T(128)} %param.12) | copy-start | bytes 196
  187.2 156.0 %all-to-all-start.1 = ((f32[16,32,128]{2,1,0:T(8,128)}), f32[16,32,128]{2,1,0:T(8,128)S(1)}, u32[]{:S(2)}, u32[]{:S(2)}) async-start(f32[16,32,128]{2,1,0:T(8,128)} %copy.128), calls=%async_computation.2 | async-start | bytes 524288 | tf_op jit(solution)/shard_map/all_to_all | solution.py:49
  190.8 110.8 %all-reduce.3.cloned.1.call-start = ((), (), s32[]{:S(2)}) async-start(), calls=%async_computation.8 | async-start | bytes 131072
  192.0 350.4 %reduce-scatter.5.cloned.1.call-start = ((), (), s32[]{:S(2)}) async-start(), calls=%async_computation.7 | async-start | bytes 393216 | tf_op jit(solution)/shard_map/reduce_scatter | solution.py:36
  632.2 6.9 copy-start.2
  640.6 13.9 %all-to-all-start.3 = ((f32[16,32,128]{2,1,0:T(8,128)}), f32[16,32,128]{2,1,0:T(8,128)S(1)}, u32[]{:S(2)}, u32[]{:S(2)}) async-start(f32[16,32,128]{2,1,0:T(8,128)} %copy.143), calls=%async_computation.5 | async-start | bytes 524288 | tf_op jit(solution)/shard_map/all_to_all | solution.py:49
Sparse Core Ops, SparseCore 0:
  83.3 5.6 reduce-scatter.2
  536.7 5.6 reduce-scatter.4
Sparse Core Ops, SparseCore 1:
  197.3 104.2 all-reduce.2
